TPU v7x, 128 devices: a whole 4x4x4 slice. The times are simulated.
128 devices in a mesh: visit: 32 (over x, y, z_lo), tx: 2 (over core), ty: 2 (over z_hi).
Axes of the slice: x: 4, y: 4, z: 4 (z_hi: 2, z_lo: 2; z = z_hi * 2 + z_lo), core: 2. Of those that a mesh axis runs over, the one named last changes fastest.
Arguments:
- images: bfloat16 [32, 16, 128, 768], P('visit', None, 'ty', 'tx'), may hold values from -8 to 8
- partners: int32 [32, 16, 2], replicated, may hold values from 0 to 31, all different within a row; in each aligned block of 16 rows (0 to 15, 16 to 31, ..., all dimensions but the last counted through in order) at most 2 rows name the same one
- coverage: int32 [32, 16, 2, 16, 96], P('visit', None, None, 'ty', 'tx'), may hold values from 0 to 1, as said below
- x_filters: bfloat16 [40, 21], replicated, may hold values from -0.359375 to 0.359375
- row_filters: bfloat16 [40, 21], replicated, may hold values from -0.359375 to 0.359375
Outputs:
- coefficients: float32 [32, 16, 2, 40], P('visit', ('tx', 'ty'))
Inputs may be any that keep to these rules, and one draw needn't show every extreme that they name: In the 16 rows of one visit no visit is named more than 2 times, and in some visit's rows one visit is named exactly 2 times; the two partners of a tile differ. `coverage`: each mask is 1 on one rectangle of blocks that holds the tile's last block row and last block column, and 0 elsewhere.
All inputs are finite; a program needn't handle non-finite values.
Results may differ from a plain program's by a relative error of at most 0.00065.
Values may be sent and summed in bfloat16 or wider, within the bound.
A program may use at most 64 MiB of HBM per device.

v0:
```python
import functools

import jax
import jax.numpy as jnp
from jax import lax
from jax.experimental import pallas as pl
from jax.experimental.pallas import tpu as pltpu
from jax.sharding import PartitionSpec as P

CAP = 2
RIDGE_TERM = 0.002
NT = (((1,), (1,)), ((), ()))
VMEM = pltpu.VMEM
ANY = pl.ANY
SMALL = pltpu.CompilerParams(vmem_limit_bytes=4 * 1024 * 1024)


def outgoing_tiles(requests, sender_visit, tile_count):
    is_sender = (requests == sender_visit).astype(jnp.int32)
    before = jnp.cumsum(is_sender, axis=1) - is_sender
    tile_ids = jnp.arange(2 * tile_count, dtype=jnp.int32)[None, :] // 2
    picked = [
        jnp.sum(jnp.where((is_sender == 1) & (before == slot), tile_ids, 0), axis=1)
        for slot in range(CAP)
    ]
    return jnp.stack(picked, axis=1).reshape(-1)


def arrival_slots(sources):
    count = sources.shape[0]
    same_source = sources[:, None] == sources[None, :]
    earlier = jnp.arange(count)[None, :] < jnp.arange(count)[:, None]
    return sources * CAP + jnp.sum((same_source & earlier).astype(jnp.int32), axis=1)


def send_pack_kernel(index_ref, tiles_ref, out_ref, sems):
    slots = out_ref.shape[0]

    def copy(slot):
        return pltpu.make_async_copy(
            tiles_ref.at[index_ref[slot]], out_ref.at[slot], sems.at[slot]
        )

    for slot in range(slots):
        copy(slot).start()
    for slot in range(slots):
        copy(slot).wait()


def send_pack(indices, tiles):
    slots = indices.shape[0]
    return pl.pallas_call(
        send_pack_kernel,
        out_shape=jax.ShapeDtypeStruct((slots,) + tiles.shape[1:], tiles.dtype),
        grid_spec=pltpu.PrefetchScalarGridSpec(
            num_scalar_prefetch=1,
            grid=(1,),
            in_specs=[pl.BlockSpec(tiles.shape, lambda i, s: (0, 0, 0))],
            out_specs=pl.BlockSpec(memory_space=pltpu.HBM),
            scratch_shapes=[pltpu.SemaphoreType.DMA((slots,))],
        ),
    )(indices, tiles)


def group_pack_kernel(index_ref, arrived_ref, out_ref, sems):
    owners, systems = out_ref.shape[0], out_ref.shape[1]
    started = []
    for owner in range(owners):
        for place in range(systems):
            number = owner * systems + place
            copy = pltpu.make_async_copy(
                arrived_ref.at[index_ref[number]], out_ref.at[owner, place], sems.at[number]
            )
            copy.start()
            started.append(copy)
    for copy in started:
        copy.wait()


def group_pack(indices, arrived, owners):
    count = indices.shape[0]
    shape = (owners, count // owners) + arrived.shape[1:]
    return pl.pallas_call(
        group_pack_kernel,
        out_shape=jax.ShapeDtypeStruct(shape, arrived.dtype),
        grid_spec=pltpu.PrefetchScalarGridSpec(
            num_scalar_prefetch=1,
            grid=(1,),
            in_specs=[pl.BlockSpec(memory_space=ANY)],
            out_specs=pl.BlockSpec(memory_space=pltpu.HBM),
            scratch_shapes=[pltpu.SemaphoreType.DMA((count,))],
        ),
        compiler_params=SMALL,
    )(indices, arrived)


def tables_kernel(half_width, x_ref, y_ref, xtab_ref, ytab_ref):
    height = 128
    r = lax.broadcasted_iota(jnp.int32, (height, 128), 0)
    l = lax.broadcasted_iota(jnp.int32, (height, 128), 1)
    near = jnp.abs(r - l) <= half_width

    def shifted(row):
        return pltpu.roll(jnp.broadcast_to(row, (height, row.shape[1])), 0, axis=1, stride=1, stride_axis=0)

    def body(pair, carry):
        for place in range(2):
            kernel = 2 * pair + place
            rows = pl.ds(pl.multiple_of(kernel * height, height), height)
            table = shifted(x_ref[pl.ds(kernel, 1), :]).astype(jnp.bfloat16)
            xtab_ref[0, rows] = table[:, :128]
            xtab_ref[1, rows] = table[:, 128:]
            table = jnp.where(near, shifted(y_ref[pl.ds(kernel, 1), :]), 0.0).astype(jnp.bfloat16)
            ytab_ref[rows] = table
        return carry

    lax.fori_loop(0, ytab_ref.shape[0] // (2 * height), body, 0)


def filter_tables(x_filters, row_filters, half_width):
    kernel_total, taps = x_filters.shape
    x_rows = jnp.pad(x_filters.astype(jnp.float32), ((0, 0), (0, 256 - taps)))
    y_rows = row_filters[:, ::-1].astype(jnp.float32)
    y_rows = jnp.concatenate(
        [y_rows[:, half_width:], jnp.zeros((kernel_total, 128 - taps), jnp.float32), y_rows[:, :half_width]], axis=1
    )
    return pl.pallas_call(
        functools.partial(tables_kernel, half_width),
        out_shape=(
            jax.ShapeDtypeStruct((2, kernel_total * 128, 128), jnp.bfloat16),
            jax.ShapeDtypeStruct((kernel_total * 128, 128), jnp.bfloat16),
        ),
    )(x_rows, y_rows)


def lane_tiles(quarter, tile_count):
    tiles = []
    for across in range(2):
        for tile in range(tile_count):
            lanes = slice(tile * 128, tile * 128 + 128)
            tiles.append(jnp.concatenate([quarter(across, 0, lanes), quarter(across, 1, lanes)], axis=0))
    return tiles


def split_dot(lhs, rhs, left):
    value = lhs if left else rhs
    total = None
    for _ in range(3):
        term = value.astype(jnp.bfloat16)
        value = value - term.astype(jnp.float32)
        part = jnp.dot(*((term, rhs) if left else (lhs, term)), preferred_element_type=jnp.float32)
        total = part if total is None else total + part
    return total


def fold(ref):
    height, width = ref.shape
    count = height // 16
    padded = -(-count // 16) * 16
    values = ref[...].reshape(count, 2, 8, width)
    sub = lax.broadcasted_iota(jnp.int32, (count, 8, width), 1)
    lane = lax.broadcasted_iota(jnp.int32, (count, 8, width), 2) % 16
    kept = jnp.where(lane == sub, values[:, 0], jnp.where(lane == sub + 8, values[:, 1], 0.0))
    kept = kept.reshape(count * 8, width)
    r = lax.broadcasted_iota(jnp.int32, (padded, count * 8), 0)
    l = lax.broadcasted_iota(jnp.int32, (padded, count * 8), 1)
    summed = split_dot((l // 8 == r).astype(jnp.bfloat16), kept, False)
    r = lax.broadcasted_iota(jnp.int32, (width, 128), 0)
    l = lax.broadcasted_iota(jnp.int32, (width, 128), 1)
    return split_dot(summed, (r // 16 == l).astype(jnp.bfloat16), True)


def normals_kernel(
    half_width, chunk, bounds_ref, template_ref, near_ref, down_ref, across_ref, far_ref, xtab_ref, ytab_ref,
    out_ref, window, science, smooth, stack, mask, first, second, third,
):
    system = pl.program_id(0)
    row_start, col_start = bounds_ref[2 * system], bounds_ref[2 * system + 1]
    rows = 128
    pairs = ytab_ref.shape[0] // 256
    kernel_total = 2 * pairs
    span = 2 * rows
    half_rows = template_ref.shape[2]
    own_tx, own_ty = bounds_ref[2 * pl.num_programs(0)], bounds_ref[2 * pl.num_programs(0) + 1]

    def template_quarter(tx, ty, lanes):
        return template_ref[2 * tx + ty, system, :, lanes]

    def science_quarter(tx, ty, lanes):
        tile = pl.ds(pl.multiple_of(system * half_rows, half_rows), half_rows)
        same = jnp.where(own_ty == ty, near_ref[tile, lanes], down_ref[tile, lanes])
        other = jnp.where(own_ty == ty, across_ref[tile, lanes], far_ref[tile, lanes])
        return jnp.where(own_tx == tx, same, other)

    tiles = lane_tiles(template_quarter, template_ref.shape[3] // 128)
    count = len(tiles)
    lane = lax.broadcasted_iota(jnp.int32, (rows, 128), 1)
    rolled = [pltpu.roll(tile.astype(jnp.float32), half_width, axis=1) for tile in tiles]
    zero = jnp.zeros((rows, 128), jnp.float32)
    for place in range(count + 1):
        before = rolled[place - 1] if place > 0 else zero
        here = rolled[place] if place < count else zero
        window[place] = jnp.where(lane < half_width, before, here).astype(jnp.bfloat16)
    for place, tile in enumerate(lane_tiles(science_quarter, template_ref.shape[3] // 128)):
        science[place] = tile

    def clear():
        first[...] = jnp.zeros_like(first)
        second[...] = jnp.zeros_like(second)
        third[...] = jnp.zeros_like(third)

    pl.when(system == 0)(clear)
    low, high, tall = 256, 512, 16 * (kernel_total + 1)

    def part_body(block, blocks):
        wide = blocks * rows
        groups = wide // 16
        c = lax.broadcasted_iota(jnp.int32, (wide, rows), 0) + block * rows
        a = lax.broadcasted_iota(jnp.int32, (wide, rows), 1)
        mask[:wide] = ((c >= col_start) & (a >= row_start)).astype(jnp.bfloat16)

        def put(start, values):
            for group in range(groups):
                stack[group, pl.ds(start, 16), :] = values[group * 16 : group * 16 + 16]

        ones = (
            lax.broadcasted_iota(jnp.int32, (wide, wide), 0)
            == lax.broadcasted_iota(jnp.int32, (wide, wide), 1)
        ).astype(jnp.bfloat16)
        own = jnp.concatenate([science[block + i] for i in range(blocks)], axis=1)
        own = lax.dot_general(ones, own, NT, preferred_element_type=jnp.float32)
        put(kernel_total * 16, own.astype(jnp.bfloat16) * mask[:wide])

        data = jnp.concatenate(
            [jnp.concatenate([window[block + i], window[block + i + 1]], axis=1) for i in range(blocks)], axis=0
        )

        def smooth_chunk(number):
            height = chunk * span
            base = number * height
            lhs = jnp.concatenate(
                [xtab_ref[0, base : base + height, :], xtab_ref[1, base : base + height, :]], axis=1
            )
            out = lax.dot_general(lhs, data, NT, preferred_element_type=jnp.float32).astype(jnp.bfloat16)
            slot = number % 2
            for i in range(blocks):
                smooth[slot, i] = out[:, i * rows : i * rows + rows]

        def basis_chunk(number):
            slot = number % 2
            for place in range(chunk):
                pair = number * chunk + place
                k1, k2 = slice(place * span, place * span + rows), slice(place * span + rows, place * span + span)
                lhs = jnp.concatenate(
                    [jnp.concatenate([smooth[slot, i, k1], smooth[slot, i, k2]], axis=1) for i in range(blocks)],
                    axis=0,
                )
                top = ytab_ref[pair * span : pair * span + rows]
                bottom = ytab_ref[pair * span + rows : pair * span + span]
                blank = jnp.zeros_like(top)
                table = jnp.concatenate(
                    [jnp.concatenate([top, blank], axis=1), jnp.concatenate([blank, bottom], axis=1)], axis=0
                )
                basis = jnp.dot(lhs, table, preferred_element_type=jnp.float32).astype(jnp.bfloat16)
                base = pair * 32 if isinstance(pair, int) else pl.multiple_of(pair * 32, 32)
                put(base, basis[:, :rows] * mask[:wide])
                put(base + 16, basis[:, rows:] * mask[:wide])

        steps = pairs // chunk
        smooth_chunk(0)
        for number in range(steps):
            if number + 1 < steps:
                smooth_chunk(number + 1)
            basis_chunk(number)

        def operand(start, stop):
            return jnp.concatenate([stack[group, start:stop, :] for group in range(groups)], axis=1)

        def gram(lhs, rhs):
            return lax.dot_general(lhs, rhs, NT, preferred_element_type=jnp.float32)

        x0, x1, x2 = operand(0, low), operand(low, high), operand(high, tall)
        second[...] += gram(jnp.concatenate([x0, x1, x2], axis=0), x1)
        first[...] += gram(jnp.concatenate([x0, x2], axis=0), x0)
        third[...] += gram(x2, x2)

    first_block = jnp.minimum(col_start // rows, count - 1)

    @pl.when(first_block % 2 == 1)
    def _():
        part_body(first_block, 1)

    def step(part, carry):
        part_body(2 * part, 2)
        return carry

    lax.fori_loop((first_block + 1) // 2, count // 2, step, 0)

    out_ref[0, 0:32] = fold(first)
    out_ref[0, 32:80] = fold(second)
    out_ref[0, 80:96] = fold(third)
    clear()


CHUNK = 4
VLIM = 24


def normals(bounds, templates, science, tables, half_width):
    owners, systems, half_rows, half_cols = templates.shape
    rows, cols = 2 * half_rows, 2 * half_cols
    span = 2 * rows
    kernel_total = tables[1].shape[0] // 128
    tall = 16 * (kernel_total + 1)
    whole = pl.BlockSpec(memory_space=VMEM)
    return pl.pallas_call(
        functools.partial(normals_kernel, half_width, CHUNK),
        out_shape=jax.ShapeDtypeStruct((systems, 96, 128), jnp.float32),
        grid_spec=pltpu.PrefetchScalarGridSpec(
            num_scalar_prefetch=1,
            grid=(systems,),
            in_specs=[
                whole, whole, whole, whole, whole,
                whole, whole,
            ],
            out_specs=pl.BlockSpec((1, 96, 128), lambda i, s: (i, 0, 0)),
            scratch_shapes=[
                VMEM((cols // 128 + 1, rows, 128), jnp.bfloat16),
                VMEM((cols // 128, rows, 128), jnp.bfloat16),
                VMEM((2, 2, CHUNK * span, rows), jnp.bfloat16),
                VMEM((span // 16, tall, rows), jnp.bfloat16),
                VMEM((span, rows), jnp.bfloat16),
                VMEM((256 + tall - 512, 256), jnp.float32),
                VMEM((tall, 256), jnp.float32),
                VMEM((tall - 512, tall - 512), jnp.float32),
            ],
        ),
        cost_estimate=pl.CostEstimate(flops=12_000_000_000, bytes_accessed=8_000_000, transcendentals=0),
        compiler_params=pltpu.CompilerParams(vmem_limit_bytes=VLIM * 1024 * 1024),
    )(bounds, templates, *science, *tables)


def solve_kernel(kernel_total, pixel_values, even_ref, odd_ref, out_ref):
    systems = 2 * even_ref.shape[0]
    r = lax.broadcasted_iota(jnp.int32, (128, 128), 0)
    l = lax.broadcasted_iota(jnp.int32, (128, 128), 1)
    matrices = []
    for system in range(systems):
        blocks = (odd_ref if system % 2 else even_ref)[system // 2]
        first, second, third = blocks[0:32], blocks[32:80], blocks[80:96]
        zero = jnp.zeros((16, 128), jnp.float32)
        left = jnp.concatenate([first[:16], zero, first[16:32]] + [zero] * 5, axis=0)
        middle = jnp.concatenate([pltpu.roll(second, 16, axis=1)] + [zero] * 5, axis=0)
        right = jnp.concatenate([zero, zero, pltpu.roll(third, 32, axis=1)] + [zero] * 5, axis=0)
        left = jnp.where((l < 16) & ((r < 16) | ((r >= 32) & (r <= kernel_total))), left, 0.0)
        middle = jnp.where((l >= 16) & (l < 32) & (r <= kernel_total), middle, 0.0)
        right = jnp.where((l >= 32) & (l <= kernel_total) & (r >= 32) & (r <= kernel_total), right, 0.0)
        known = left + middle + right
        other = jnp.transpose(known)
        absent = ((r >= 16) & (r < 32) & (l < 16)) | ((l >= 32) & (r < 32))
        whole = jnp.where(absent, other, known) / pixel_values
        whole = whole + jnp.where((r == l) & (r < kernel_total), RIDGE_TERM, 0.0)
        matrices.append(whole[:kernel_total])
    width = kernel_total + 1
    beside = 128 // width
    groups = []
    for start in range(0, systems, beside):
        total = matrices[start]
        for place in range(1, min(beside, systems - start)):
            total = total + pltpu.roll(matrices[start + place], place * width, axis=1)
        groups.append(total)
    row_ids = lax.broadcasted_iota(jnp.int32, (kernel_total, 128), 0)
    base = lax.broadcasted_iota(jnp.int32, (kernel_total, 128), 1) // width * width
    for pivot in range(0, kernel_total, 2):
        place, after = jnp.minimum(base + pivot, 127), jnp.minimum(base + pivot + 1, 127)
        for number, work in enumerate(groups):
            real = base[:1] < min(beside, systems - number * beside) * width
            left, right = jnp.take_along_axis(work, place, axis=1), jnp.take_along_axis(work, after, axis=1)
            top, bottom = work[pivot : pivot + 1], work[pivot + 1 : pivot + 2]
            head = jnp.where(real, left[pivot : pivot + 1], 1.0)
            ratio = right[pivot : pivot + 1] / head
            lower = left[pivot + 1 : pivot + 2]
            top = top / head
            tail = jnp.where(real, right[pivot + 1 : pivot + 2] - lower * ratio, 1.0)
            bottom = (bottom - lower * top) / tail
            top = top - ratio * bottom
            work = work - left * top - right * bottom
            groups[number] = jnp.where(row_ids == pivot, top, jnp.where(row_ids == pivot + 1, bottom, work))
    for number, work in enumerate(groups):
        turned = jnp.transpose(jnp.concatenate([work, jnp.zeros((128 - kernel_total, 128), jnp.float32)], axis=0))
        for place in range(min(beside, systems - number * beside)):
            last = place * width + kernel_total
            out_ref[number * beside + place : number * beside + place + 1] = turned[last : last + 1, :kernel_total]


def solve(even, odd, kernel_total, pixel_values):
    return pl.pallas_call(
        functools.partial(solve_kernel, kernel_total, float(pixel_values)),
        out_shape=jax.ShapeDtypeStruct((2 * even.shape[0], kernel_total), jnp.float32),
        compiler_params=SMALL,
    )(even, odd)


def body(images, partners, coverage, x_filters, row_filters):
    visit = lax.axis_index("visit")
    own_tiles = images[0]
    tile_count, row_count, col_count = own_tiles.shape
    half_width = (x_filters.shape[1] - 1) // 2
    kernel_total = x_filters.shape[0]
    visit_count = partners.shape[0]
    owners = lax.axis_size("tx") * lax.axis_size("ty")
    requests = partners.reshape(visit_count, 2 * tile_count)
    own_requests = lax.dynamic_index_in_dim(requests, visit, 0, keepdims=False)
    share = tile_count // owners
    group = ("tx", "ty")
    sent = send_pack(outgoing_tiles(requests, visit, tile_count), own_tiles)
    arrived = lax.all_to_all(
        sent.reshape((visit_count, CAP) + own_tiles.shape[1:]), "visit", split_axis=0, concat_axis=0, tiled=True
    )
    arrived = arrived.reshape((visit_count * CAP,) + own_tiles.shape[1:])

    blocks = coverage[0]
    block_size = row_count // blocks.shape[2]
    row_blocks = jnp.max(blocks, axis=3).sum(axis=2)
    col_blocks = jnp.max(blocks, axis=2).sum(axis=2)
    counts = jnp.stack([row_blocks, col_blocks], axis=-1).reshape(owners, 2 * share, 2).astype(own_tiles.dtype)
    counts = jnp.pad(counts, ((0, 0), (0, 16 - 2 * share), (0, col_count - 2)))
    science = jnp.concatenate([own_tiles.reshape(owners, share * row_count, col_count), counts], axis=1)
    tx, ty = lax.axis_index("tx"), lax.axis_index("ty")
    parts, row_blocks, col_blocks = [], 0.0, 0.0
    for dx in range(2):
        for dy in range(2):
            peer_x, peer_y = (tx + dx) % 2, (ty + dy) % 2
            part = lax.dynamic_index_in_dim(science, 2 * peer_x + peer_y, 0, keepdims=False)
            if dx or dy:
                swap = 2 * dx + dy
                part = lax.ppermute(part, group, [(i, i ^ swap) for i in range(owners)])
            parts.append(part)
            tally = part[share * row_count : share * row_count + 2 * share, :2].astype(jnp.float32)
            row_blocks += jnp.where(peer_x == 1, tally[:, 0], 0.0)
            col_blocks += jnp.where(peer_y == 1, tally[:, 1], 0.0)
    row_start = 2 * row_count - block_size * row_blocks
    col_start = 2 * col_count - block_size * col_blocks
    bounds = jnp.stack([row_start, col_start], axis=-1).astype(jnp.int32).reshape(share, 2, 2)
    place = jnp.stack([tx, ty]).astype(jnp.int32)

    slots = arrival_slots(own_requests).reshape(tile_count, 2)
    pixel_values = row_count * col_count * owners
    grouped = [group_pack(slots[:, partner], arrived, owners) for partner in range(2)]
    tables = filter_tables(x_filters, row_filters, half_width)
    sums = []
    for partner in range(2):
        templates = lax.all_to_all(grouped[partner], group, split_axis=0, concat_axis=0, tiled=True)
        limits = jnp.concatenate([bounds[:, partner].reshape(-1), place])
        sums.append(normals(limits, templates, parts, tables, half_width))
    coefficients = solve(*sums, kernel_total, pixel_values)
    return coefficients.reshape(1, tile_count // owners, 2, kernel_total)


def solution(mesh):
    return jax.shard_map(
        body,
        mesh=mesh,
        in_specs=(P("visit", None, "ty", "tx"), P(), P("visit", None, None, "ty", "tx"), P(), P()),
        out_specs=P("visit", ("tx", "ty"), None, None),
        check_vma=False,
    )
```

profile of v0, /device:TPU:50, one launch (start us, length us, event | category | flops | bytes accessed | tf_op | source)
XLA Modules:
  0.0 167.1 jit_solution(13834270430190889523)
XLA Ops:
  0.0 0.8 copy.41
  0.8 0.2 reduce_window_sum.13
  1.1 0.8 fusion.2
  1.9 0.1 copy.44
  2.0 0.6 reshape.84.index_ref
  2.6 4.0 %shard_map.55 = bf16[64,64,384]{2,1,0:T(8,128)(2,1)} custom-call(s32[64]{0:T(128)} %reshape.84.index_ref, bf16[16,64,384]{2,1,0:T(8,128)(2,1)} %bitcast.28), custom_call_target="tpu_custom_call" | custom-call | tf_op jit(solution)/shard_map/pallas_call | solution.py:52
  6.7 8.4 %all-to-all-start = ((bf16[32,2,64,384]{3,2,1,0:T(8,128)(2,1)}), bf16[32,2,64,384]{3,2,1,0:T(8,128)(2,1)S(1)}, u32[]{:S(2)}, u32[]{:S(2)}) async-start(bf16[32,2,64,384]{3,2,1,0:T(8,128)(2,1)} %bitcast.27), calls=%async_computation | async-start | bytes 6291456 | tf_op jit(solution)/shard_map/all_to_all | solution.py:417
  15.2 0.7 fusion.9
  15.9 0.3 reduce_sum.47
  16.2 0.3 reduce_sum.48
  16.6 0.1 stack.34
  16.8 0.1 copy.50
  16.9 1.2 fusion.1
  18.1 0.9 dynamic-slice_bitcast_fusion.3
  19.0 1.9 %collective-permute-start.2 = (bf16[272,384]{1,0:T(8,128)(2,1)}, bf16[272,384]{1,0:T(8,128)(2,1)}, u32[]{:S(2)}, u32[]{:S(2)}) collective-permute-start(bf16[272,384]{1,0:T(8,128)(2,1)} %get-tuple-element.18), channel_id=1, source_target_pairs={{0,3},{1,2},{2,1},{3,0},{4,7},{5,6},{6,5},{7,4},{8,11},{9,10},{10,... | collective-permute-start | bytes 626696 | tf_op jit(solution)/shard_map/ppermute | solution.py:437
  20.9 1.2 collective-permute-start.1
  22.1 0.6 collective-permute-start
  22.7 0.1 copy.46
  22.8 0.1 rev.3
  22.9 0.1 copy.45
  23.1 0.2 convert_reduce_fusion
  23.3 0.1 mul.34
  23.5 0.6 pad_convert_fusion.x_ref
  24.1 0.7 pad_maximum_fusion.y_ref
  24.8 5.3 %shard_map.57 = (bf16[2,5120,128]{2,1,0:T(8,128)(2,1)}, bf16[5120,128]{1,0:T(8,128)(2,1)}) custom-call(f32[40,256]{1,0:T(8,128)} %pad_convert_fusion.x_ref, f32[40,128]{1,0:T(8,128)} %pad_maximum_fusion.y_ref), custom_call_target="tpu_custom_call" | custom-call | tf_op jit(solution)/shard_map/pallas_call | solution.py:127
  30.1 0.2 slice_reduce_fusion
  30.3 26.3 %collective-permute-done.2.far_ref = bf16[272,384]{1,0:T(8,128)(2,1)} collective-permute-done((bf16[272,384]{1,0:T(8,128)(2,1)}, bf16[272,384]{1,0:T(8,128)(2,1)}, u32[]{:S(2)}, u32[]{:S(2)}) %collective-permute-start.2) | collective-permute-done | bytes 208928 | tf_op jit(solution)/shard_map/ppermute | solution.py:437
  56.5 0.7 slice_convert_fusion
  57.2 0.7 slice_convert_fusion.1
  57.9 1.8 %shard_map.59 = bf16[4,4,64,384]{3,2,1,0:T(8,128)(2,1)S(1)} custom-call(s32[16]{0:T(128)S(1)} %get-tuple-element.15.index_ref, bf16[64,64,384]{2,1,0:T(8,128)(2,1)S(1)} %bitcast.25), custom_call_target="tpu_custom_call" | custom-call | tf_op jit(solution)/shard_map/pallas_call | solution.py:83
  59.7 0.9 copy-done
  60.5 4.2 %all-to-all-start.2 = ((bf16[4,4,64,384]{3,2,1,0:T(8,128)(2,1)}), bf16[4,4,64,384]{3,2,1,0:T(8,128)(2,1)}, u32[]{:S(2)}, u32[]{:S(2)}) async-start(bf16[4,4,64,384]{3,2,1,0:T(8,128)(2,1)} %copy-done), calls=%async_computation.2 | async-start | bytes 1572864 | tf_op jit(solution)/shard_map/all_to_all | solution.py:453
  64.7 0.7 slice_convert_fusion.2
  65.4 0.2 subtract_reduce_fusion.1
  65.9 0.1 copy.47
  66.0 0.1 reshape_squeeze.11
  66.0 0.1 copy.40
  66.2 0.1 reshape_squeeze.10
  66.3 1.8 %shard_map.56 = bf16[4,4,64,384]{3,2,1,0:T(8,128)(2,1)S(1)} custom-call(s32[16]{0:T(128)S(1)} %get-tuple-element.16.index_ref, bf16[64,64,384]{2,1,0:T(8,128)(2,1)S(1)} %bitcast.26), custom_call_target="tpu_custom_call" | custom-call | tf_op jit(solution)/shard_map/pallas_call | solution.py:83
  68.1 0.9 copy-done.1
  69.0 8.9 %all-to-all-done.2.template_ref = bf16[4,4,64,384]{3,2,1,0:T(8,128)(2,1)} async-done(((bf16[4,4,64,384]{3,2,1,0:T(8,128)(2,1)}), bf16[4,4,64,384]{3,2,1,0:T(8,128)(2,1)}, u32[]{:S(2)}, u32[]{:S(2)}) %all-to-all-start.2) | async-done | bytes 786464 | tf_op jit(solution)/shard_map/all_to_all | solution.py:453
  77.9 4.4 %all-to-all-start.1 = ((bf16[4,4,64,384]{3,2,1,0:T(8,128)(2,1)}), bf16[4,4,64,384]{3,2,1,0:T(8,128)(2,1)}, u32[]{:S(2)}, u32[]{:S(2)}) async-start(bf16[4,4,64,384]{3,2,1,0:T(8,128)(2,1)} %copy-done.1), calls=%async_computation.1 | async-start | bytes 1572864 | tf_op jit(solution)/shard_map/all_to_all | solution.py:453
  82.3 1.7 %copy-done.2 = bf16[2,5120,128]{2,1,0:T(8,128)(2,1)S(1)} copy-done((bf16[2,5120,128]{2,1,0:T(8,128)(2,1)S(1)}, bf16[2,5120,128]{2,1,0:T(8,128)(2,1)}, u32[]{:S(2)}) %copy-start.2) | copy-done | bytes 2621464
  84.0 1.3 copy-done.3
  85.4 35.6 %shard_map.60.odd_ref = f32[4,96,128]{2,1,0:T(8,128)S(1)} custom-call(s32[10]{0:T(128)S(1)} %get-tuple-element.26.bounds_ref, bf16[4,4,64,384]{3,2,1,0:T(8,128)(2,1)} %all-to-all-done.2.template_ref, bf16[272,384]{1,0:T(8,128)(2,1)S(1)} %get-tuple-element.17.near_ref, bf16[272,384]{1,0:T(8,128)(2,1)} %collective-permute-done.down_ref, ...), custom_call_target="tpu_custom_call" | custom-call | flops 12000000000 | bytes 8000000 | tf_op jit(solution)/shard_map/pallas_call | solution.py:316
  120.9 1.3 copy-done.4
  122.3 41.6 %shard_map.58.even_ref = f32[4,96,128]{2,1,0:T(8,128)S(1)} custom-call(s32[10]{0:T(128)S(1)} %get-tuple-element.25.bounds_ref, bf16[4,4,64,384]{3,2,1,0:T(8,128)(2,1)} %all-to-all-done.1.template_ref, bf16[272,384]{1,0:T(8,128)(2,1)S(1)} %get-tuple-element.17.near_ref, bf16[272,384]{1,0:T(8,128)(2,1)} %collective-permute-done.down_ref, ...), custom_call_target="tpu_custom_call" | custom-call | flops 12000000000 | bytes 8000000 | tf_op jit(solution)/shard_map/pallas_call | solution.py:316
  163.9 3.3 %shard_map.61 = f32[8,40]{1,0:T(8,128)} custom-call(f32[4,96,128]{2,1,0:T(8,128)S(1)} %shard_map.58.even_ref, f32[4,96,128]{2,1,0:T(8,128)S(1)} %shard_map.60.odd_ref), custom_call_target="tpu_custom_call" | custom-call | tf_op jit(solution)/shard_map/pallas_call | solution.py:397
  (36 shorter events, 0.9 us)
Async XLA Ops:
  6.7 8.5 %copy-start.5 = (s32[1,16,2,8,48]{4,3,2,1,0:T(8,128)S(1)}, s32[1,16,2,8,48]{4,3,2,1,0:T(8,128)}, u32[]{:S(2)}) copy-start(s32[1,16,2,8,48]{4,3,2,1,0:T(8,128)} %param.7) | copy-start | bytes 147460
  6.7 51.2 %all-to-all-start = ((bf16[32,2,64,384]{3,2,1,0:T(8,128)(2,1)}), bf16[32,2,64,384]{3,2,1,0:T(8,128)(2,1)S(1)}, u32[]{:S(2)}, u32[]{:S(2)}) async-start(bf16[32,2,64,384]{3,2,1,0:T(8,128)(2,1)} %bitcast.27), calls=%async_computation | async-start | bytes 6291456 | tf_op jit(solution)/shard_map/all_to_all | solution.py:417
  16.8 5.9 %copy-start.6 = (bf16[40,21]{0,1:T(8,128)(2,1)S(1)}, bf16[40,21]{0,1:T(8,128)(2,1)}, u32[]{:S(2)}) copy-start(bf16[40,21]{0,1:T(8,128)(2,1)} %param.9) | copy-start | bytes 5044
  16.9 6.1 %copy-start.7 = (bf16[40,21]{0,1:T(8,128)(2,1)S(1)}, bf16[40,21]{0,1:T(8,128)(2,1)}, u32[]{:S(2)}) copy-start(bf16[40,21]{0,1:T(8,128)(2,1)} %param.8) | copy-start | bytes 5044
  19.0 37.5 %collective-permute-start.2 = (bf16[272,384]{1,0:T(8,128)(2,1)}, bf16[272,384]{1,0:T(8,128)(2,1)}, u32[]{:S(2)}, u32[]{:S(2)}) collective-permute-start(bf16[272,384]{1,0:T(8,128)(2,1)} %get-tuple-element.18), channel_id=1, source_target_pairs={{0,3},{1,2},{2,1},{3,0},{4,7},{5,6},{6,5},{7,4},{8,11},{9,10},{10,... | collective-permute-start | bytes 626696 | tf_op jit(solution)/shard_map/ppermute | solution.py:437
  20.9 36.3 %collective-permute-start.1 = (bf16[272,384]{1,0:T(8,128)(2,1)}, bf16[272,384]{1,0:T(8,128)(2,1)}, u32[]{:S(2)}, u32[]{:S(2)}) collective-permute-start(bf16[272,384]{1,0:T(8,128)(2,1)} %get-tuple-element.19), channel_id=1, source_target_pairs={{0,2},{1,3},{2,0},{3,1},{4,6},{5,7},{6,4},{7,5},{8,10},{9,11},{10,... | collective-permute-start | bytes 626696 | tf_op jit(solution)/shard_map/ppermute | solution.py:437
  22.1 42.6 %collective-permute-start = (bf16[272,384]{1,0:T(8,128)(2,1)}, bf16[272,384]{1,0:T(8,128)(2,1)}, u32[]{:S(2)}, u32[]{:S(2)}) collective-permute-start(bf16[272,384]{1,0:T(8,128)(2,1)} %get-tuple-element.20), channel_id=1, source_target_pairs={{0,1},{1,0},{2,3},{3,2},{4,5},{5,4},{6,7},{7,6},{8,9},{9,8},{10,11... | collective-permute-start | bytes 626696 | tf_op jit(solution)/shard_map/ppermute | solution.py:437
  59.7 0.9 copy-start
  60.5 17.4 %all-to-all-start.2 = ((bf16[4,4,64,384]{3,2,1,0:T(8,128)(2,1)}), bf16[4,4,64,384]{3,2,1,0:T(8,128)(2,1)}, u32[]{:S(2)}, u32[]{:S(2)}) async-start(bf16[4,4,64,384]{3,2,1,0:T(8,128)(2,1)} %copy-done), calls=%async_computation.2 | async-start | bytes 1572864 | tf_op jit(solution)/shard_map/all_to_all | solution.py:453
  68.1 0.9 copy-start.1
  77.9 43.0 %all-to-all-start.1 = ((bf16[4,4,64,384]{3,2,1,0:T(8,128)(2,1)}), bf16[4,4,64,384]{3,2,1,0:T(8,128)(2,1)}, u32[]{:S(2)}, u32[]{:S(2)}) async-start(bf16[4,4,64,384]{3,2,1,0:T(8,128)(2,1)} %copy-done.1), calls=%async_computation.1 | async-start | bytes 1572864 | tf_op jit(solution)/shard_map/all_to_all | solution.py:453
  82.3 1.7 %copy-start.2 = (bf16[2,5120,128]{2,1,0:T(8,128)(2,1)S(1)}, bf16[2,5120,128]{2,1,0:T(8,128)(2,1)}, u32[]{:S(2)}) copy-start(bf16[2,5120,128]{2,1,0:T(8,128)(2,1)} %get-tuple-element.7.xtab_ref) | copy-start | bytes 7864324
  84.0 1.3 copy-start.3
  120.9 1.3 copy-start.4
where the time goes:
time: 167 us
  Pallas kernels  93.3 us (56%)
  waiting for transfers between devices  35.2 us (21%)
  starting transfers between devices  20.6 us (12%)
  local copies, waits for them, and re-layouts  10.3 us (6%)
  other arithmetic  7.45 us (4%)
    pallas_call x2, Pallas kernels, normals(): pl.pallas_call(functools.partial(normals_kernel, half_width, CHUNK), out_...  77.2 us
    ppermute x3, waiting for transfers between devices, body(): part = lax.ppermute(part, group, [(i, i ^ swap) for i in range(owners)])  26.3 us
    all_to_all x2, waiting for transfers between devices, body(): lax.all_to_all(grouped[partner], group, split_axis=0, concat_axis=0, tile...  8.89 us
    all_to_all x2, starting transfers between devices, body(): lax.all_to_all(grouped[partner], group, split_axis=0, concat_axis=0, tile...  8.56 us
    all_to_all x1, starting transfers between devices, body(): lax.all_to_all(sent.reshape((visit_count, CAP) + own_tiles.shape[1:]), 'v...  8.44 us
    unnamed x19, local copies, waits for them, and re-layouts  6.45 us
    pallas_call x1, Pallas kernels, filter_tables(): pl.pallas_call(functools.partial(tables_kernel, half_width), out_shape=(j...  5.26 us
    pallas_call x1, Pallas kernels, send_pack(): pl.pallas_call(send_pack_kernel, out_shape=jax.ShapeDtypeStruct((slots,)...  4.03 us
  transfers between devices with their start and end apart: 6, of which 2 were waited for; matrix products, arithmetic and copies ran while one was open for 5% of the time, Pallas kernels for 27%

commit v1 on v0

--- a/solution.py
+++ b/solution.py
@@ -117,7 +117,12 @@
     lax.fori_loop(0, ytab_ref.shape[0] // (2 * height), body, 0)
 
 
-def filter_tables(x_filters, row_filters, half_width):
+def pass_kernel(x_ref, y_ref, x_out, y_out):
+    x_out[...] = x_ref[...]
+    y_out[...] = y_ref[...]
+
+
+def filter_rows(x_filters, row_filters, half_width):
     kernel_total, taps = x_filters.shape
     x_rows = jnp.pad(x_filters.astype(jnp.float32), ((0, 0), (0, 256 - taps)))
     y_rows = row_filters[:, ::-1].astype(jnp.float32)
@@ -125,11 +130,28 @@
         [y_rows[:, half_width:], jnp.zeros((kernel_total, 128 - taps), jnp.float32), y_rows[:, :half_width]], axis=1
     )
     return pl.pallas_call(
+        pass_kernel,
+        out_shape=(
+            jax.ShapeDtypeStruct(x_rows.shape, jnp.float32),
+            jax.ShapeDtypeStruct(y_rows.shape, jnp.float32),
+        ),
+        cost_estimate=pl.CostEstimate(flops=HINT, bytes_accessed=120_000, transcendentals=0),
+        compiler_params=SMALL,
+    )(x_rows, y_rows)
+
+
+HINT = 8_000_000_000
+
+
+def filter_tables(x_rows, y_rows, half_width):
+    kernel_total = x_rows.shape[0]
+    return pl.pallas_call(
         functools.partial(tables_kernel, half_width),
         out_shape=(
             jax.ShapeDtypeStruct((2, kernel_total * 128, 128), jnp.bfloat16),
             jax.ShapeDtypeStruct((kernel_total * 128, 128), jnp.bfloat16),
         ),
+        compiler_params=pltpu.CompilerParams(vmem_limit_bytes=12 * 1024 * 1024),
     )(x_rows, y_rows)
 
 
@@ -447,7 +469,9 @@
     slots = arrival_slots(own_requests).reshape(tile_count, 2)
     pixel_values = row_count * col_count * owners
     grouped = [group_pack(slots[:, partner], arrived, owners) for partner in range(2)]
-    tables = filter_tables(x_filters, row_filters, half_width)
+    filters = filter_rows(x_filters, row_filters, half_width)
+    *filters, _ = lax.optimization_barrier((*filters, grouped[0]))
+    tables = filter_tables(*filters, half_width)
     sums = []
     for partner in range(2):
         templates = lax.all_to_all(grouped[partner], group, split_axis=0, concat_axis=0, tiled=True)

time: 167 us -> 164 us (0.982)
  the two profiles are of different devices: /device:TPU:50 before, /device:TPU:75 now
where the time goes in v1:
time: 164 us; the launch traced here: 161 us
  Pallas kernels  85.5 us (52%)
  waiting for transfers between devices  32.4 us (20%)
  starting transfers between devices  26.7 us (16%)
  local copies, waits for them, and re-layouts  9.66 us (6%)
  other arithmetic  6.22 us (4%)
    pallas_call x2, Pallas kernels, normals(): pl.pallas_call(functools.partial(normals_kernel, half_width, CHUNK), out_...  72.1 us
    ppermute x3, waiting for transfers between devices, body(): part = lax.ppermute(part, group, [(i, i ^ swap) for i in range(owners)])  30.1 us
    all_to_all x2, starting transfers between devices, body(): lax.all_to_all(grouped[partner], group, split_axis=0, concat_axis=0, tile...  14.5 us
    all_to_all x1, starting transfers between devices, body(): lax.all_to_all(sent.reshape((visit_count, CAP) + own_tiles.shape[1:]), 'v...  8.15 us
    unnamed x19, local copies, waits for them, and re-layouts  5.82 us
    ppermute x3, starting transfers between devices, body(): part = lax.ppermute(part, group, [(i, i ^ swap) for i in range(owners)])  4.09 us
    pallas_call x1, Pallas kernels, send_pack(): pl.pallas_call(send_pack_kernel, out_shape=jax.ShapeDtypeStruct((slots,)...  4.03 us
    pallas_call x2, Pallas kernels, group_pack(): pl.pallas_call(group_pack_kernel, out_shape=jax.ShapeDtypeStruct(shape, a...  3.59 us
  transfers between devices with their start and end apart: 6, of which 2 were waited for; matrix products, arithmetic and copies ran while one was open for 5% of the time, Pallas kernels for 25%

profile of v1, /device:TPU:75, one launch (start us, length us, event | category | flops | bytes accessed | tf_op | source)
XLA Modules:
  0.0 160.8 jit_solution(4588555713384113337)
XLA Ops:
  0.0 0.8 copy.41
  0.8 0.2 reduce_window_sum.13
  1.1 0.8 fusion.2
  1.9 0.1 copy.44
  2.0 0.6 reshape.84.index_ref
  2.6 4.0 %shard_map.55 = bf16[64,64,384]{2,1,0:T(8,128)(2,1)} custom-call(s32[64]{0:T(128)} %reshape.84.index_ref, bf16[16,64,384]{2,1,0:T(8,128)(2,1)} %bitcast.28), custom_call_target="tpu_custom_call" | custom-call | tf_op jit(solution)/shard_map/pallas_call | solution.py:52
  6.7 8.2 %all-to-all-start = ((bf16[32,2,64,384]{3,2,1,0:T(8,128)(2,1)}), bf16[32,2,64,384]{3,2,1,0:T(8,128)(2,1)S(1)}, u32[]{:S(2)}, u32[]{:S(2)}) async-start(bf16[32,2,64,384]{3,2,1,0:T(8,128)(2,1)} %bitcast.27), calls=%async_computation | async-start | bytes 6291456 | tf_op jit(solution)/shard_map/all_to_all | solution.py:439
  14.9 0.7 fusion.9
  15.6 0.3 reduce_sum.47
  15.9 0.3 reduce_sum.48
  16.3 0.1 stack.34
  16.4 0.1 stack.35
  16.5 0.1 copy.50
  16.6 1.2 fusion.1
  17.8 0.9 dynamic-slice_bitcast_fusion.3
  18.7 0.8 collective-permute-start.2
  19.5 0.5 collective-permute-start.1
  19.9 2.9 %collective-permute-start = (bf16[272,384]{1,0:T(8,128)(2,1)}, bf16[272,384]{1,0:T(8,128)(2,1)}, u32[]{:S(2)}, u32[]{:S(2)}) collective-permute-start(bf16[272,384]{1,0:T(8,128)(2,1)} %get-tuple-element.28), channel_id=1, source_target_pairs={{0,1},{1,0},{2,3},{3,2},{4,5},{5,4},{6,7},{7,6},{8,9},{9,8},{10,11... | collective-permute-start | bytes 626696 | tf_op jit(solution)/shard_map/ppermute | solution.py:459
  22.8 0.1 copy.46
  22.9 0.1 rev.3
  23.1 0.1 copy.45
  23.2 0.2 convert_reduce_fusion
  23.5 0.1 mul.34
  23.6 0.2 slice_reduce_fusion
  23.9 30.1 %collective-permute-done.2.far_ref = bf16[272,384]{1,0:T(8,128)(2,1)} collective-permute-done((bf16[272,384]{1,0:T(8,128)(2,1)}, bf16[272,384]{1,0:T(8,128)(2,1)}, u32[]{:S(2)}, u32[]{:S(2)}) %collective-permute-start.2) | collective-permute-done | bytes 208928 | tf_op jit(solution)/shard_map/ppermute | solution.py:459
  54.1 0.7 slice_convert_fusion
  54.8 0.7 slice_convert_fusion.1
  55.4 1.8 %shard_map.60 = bf16[4,4,64,384]{3,2,1,0:T(8,128)(2,1)S(1)} custom-call(s32[16]{0:T(128)S(1)} %get-tuple-element.23.index_ref, bf16[64,64,384]{2,1,0:T(8,128)(2,1)S(1)} %bitcast.25), custom_call_target="tpu_custom_call" | custom-call | tf_op jit(solution)/shard_map/pallas_call | solution.py:83
  57.2 0.9 copy-done
  58.2 7.2 %all-to-all-start.2 = ((bf16[4,4,64,384]{3,2,1,0:T(8,128)(2,1)}), bf16[4,4,64,384]{3,2,1,0:T(8,128)(2,1)}, u32[]{:S(2)}, u32[]{:S(2)}) async-start(bf16[4,4,64,384]{3,2,1,0:T(8,128)(2,1)} %copy-done), calls=%async_computation.2 | async-start | bytes 1572864 | tf_op jit(solution)/shard_map/all_to_all | solution.py:477
  65.4 0.7 slice_convert_fusion.2
  66.0 0.2 subtract_reduce_fusion.1
  66.2 0.1 stack.37
  66.5 0.1 copy.47
  66.6 0.1 reshape_squeeze.11
  66.7 0.1 copy.40
  66.8 0.1 reshape_squeeze.10
  67.0 1.8 %shard_map.56 = bf16[4,4,64,384]{3,2,1,0:T(8,128)(2,1)S(1)} custom-call(s32[16]{0:T(128)S(1)} %get-tuple-element.24.index_ref, bf16[64,64,384]{2,1,0:T(8,128)(2,1)S(1)} %bitcast.26), custom_call_target="tpu_custom_call" | custom-call | tf_op jit(solution)/shard_map/pallas_call | solution.py:83
  68.8 0.9 copy-done.1
  69.6 2.5 %shard_map.58 = (bf16[2,5120,128]{2,1,0:T(8,128)(2,1)S(1)}, bf16[5120,128]{1,0:T(8,128)(2,1)S(1)}) custom-call(f32[40,256]{1,0:T(8,128)S(1)} %get-tuple-element.13.x_ref, f32[40,128]{1,0:T(8,128)S(1)} %get-tuple-element.14.y_ref), custom_call_target="tpu_custom_call" | custom-call | tf_op jit(solution)/shard_map/pallas_call | solution.py:148
  72.2 1.1 copy-done.2
  73.2 2.3 %all-to-all-done.2.template_ref = bf16[4,4,64,384]{3,2,1,0:T(8,128)(2,1)} async-done(((bf16[4,4,64,384]{3,2,1,0:T(8,128)(2,1)}), bf16[4,4,64,384]{3,2,1,0:T(8,128)(2,1)}, u32[]{:S(2)}, u32[]{:S(2)}) %all-to-all-start.2) | async-done | bytes 786464 | tf_op jit(solution)/shard_map/all_to_all | solution.py:477
  75.5 7.3 %all-to-all-start.1 = ((bf16[4,4,64,384]{3,2,1,0:T(8,128)(2,1)}), bf16[4,4,64,384]{3,2,1,0:T(8,128)(2,1)}, u32[]{:S(2)}, u32[]{:S(2)}) async-start(bf16[4,4,64,384]{3,2,1,0:T(8,128)(2,1)} %copy-done.1), calls=%async_computation.1 | async-start | bytes 1572864 | tf_op jit(solution)/shard_map/all_to_all | solution.py:477
  82.8 1.3 copy-done.3
  84.1 34.5 %shard_map.61.odd_ref = f32[4,96,128]{2,1,0:T(8,128)S(1)} custom-call(s32[10]{0:T(128)S(1)} %get-tuple-element.34.bounds_ref, bf16[4,4,64,384]{3,2,1,0:T(8,128)(2,1)} %all-to-all-done.2.template_ref, bf16[272,384]{1,0:T(8,128)(2,1)S(1)} %get-tuple-element.25.near_ref, bf16[272,384]{1,0:T(8,128)(2,1)} %collective-permute-done.down_ref, ...), custom_call_target="tpu_custom_call" | custom-call | flops 12000000000 | bytes 8000000 | tf_op jit(solution)/shard_map/pallas_call | solution.py:338
  118.6 1.3 copy-done.4
  120.0 37.6 %shard_map.59.even_ref = f32[4,96,128]{2,1,0:T(8,128)S(1)} custom-call(s32[10]{0:T(128)S(1)} %get-tuple-element.33.bounds_ref, bf16[4,4,64,384]{3,2,1,0:T(8,128)(2,1)} %all-to-all-done.1.template_ref, bf16[272,384]{1,0:T(8,128)(2,1)S(1)} %get-tuple-element.25.near_ref, bf16[272,384]{1,0:T(8,128)(2,1)} %collective-permute-done.down_ref, ...), custom_call_target="tpu_custom_call" | custom-call | flops 12000000000 | bytes 8000000 | tf_op jit(solution)/shard_map/pallas_call | solution.py:338
  157.5 3.3 %shard_map.62 = f32[8,40]{1,0:T(8,128)} custom-call(f32[4,96,128]{2,1,0:T(8,128)S(1)} %shard_map.59.even_ref, f32[4,96,128]{2,1,0:T(8,128)S(1)} %shard_map.61.odd_ref), custom_call_target="tpu_custom_call" | custom-call | tf_op jit(solution)/shard_map/pallas_call | solution.py:419
  (37 shorter events, 0.8 us)
Async XLA Ops:
  6.7 8.2 %copy-start.5 = (s32[1,16,2,8,48]{4,3,2,1,0:T(8,128)S(1)}, s32[1,16,2,8,48]{4,3,2,1,0:T(8,128)}, u32[]{:S(2)}) copy-start(s32[1,16,2,8,48]{4,3,2,1,0:T(8,128)} %param.7) | copy-start | bytes 147460
  6.7 48.7 %all-to-all-start = ((bf16[32,2,64,384]{3,2,1,0:T(8,128)(2,1)}), bf16[32,2,64,384]{3,2,1,0:T(8,128)(2,1)S(1)}, u32[]{:S(2)}, u32[]{:S(2)}) async-start(bf16[32,2,64,384]{3,2,1,0:T(8,128)(2,1)} %bitcast.27), calls=%async_computation | async-start | bytes 6291456 | tf_op jit(solution)/shard_map/all_to_all | solution.py:439
  16.5 6.3 %copy-start.6 = (bf16[40,21]{0,1:T(8,128)(2,1)S(1)}, bf16[40,21]{0,1:T(8,128)(2,1)}, u32[]{:S(2)}) copy-start(bf16[40,21]{0,1:T(8,128)(2,1)} %param.9) | copy-start | bytes 5044
  16.6 6.5 %copy-start.7 = (bf16[40,21]{0,1:T(8,128)(2,1)S(1)}, bf16[40,21]{0,1:T(8,128)(2,1)}, u32[]{:S(2)}) copy-start(bf16[40,21]{0,1:T(8,128)(2,1)} %param.8) | copy-start | bytes 5044
  18.7 35.4 %collective-permute-start.2 = (bf16[272,384]{1,0:T(8,128)(2,1)}, bf16[272,384]{1,0:T(8,128)(2,1)}, u32[]{:S(2)}, u32[]{:S(2)}) collective-permute-start(bf16[272,384]{1,0:T(8,128)(2,1)} %get-tuple-element.26), channel_id=1, source_target_pairs={{0,3},{1,2},{2,1},{3,0},{4,7},{5,6},{6,5},{7,4},{8,11},{9,10},{10,... | collective-permute-start | bytes 626696 | tf_op jit(solution)/shard_map/ppermute | solution.py:459
  19.5 35.3 %collective-permute-start.1 = (bf16[272,384]{1,0:T(8,128)(2,1)}, bf16[272,384]{1,0:T(8,128)(2,1)}, u32[]{:S(2)}, u32[]{:S(2)}) collective-permute-start(bf16[272,384]{1,0:T(8,128)(2,1)} %get-tuple-element.27), channel_id=1, source_target_pairs={{0,2},{1,3},{2,0},{3,1},{4,6},{5,7},{6,4},{7,5},{8,10},{9,11},{10,... | collective-permute-start | bytes 626696 | tf_op jit(solution)/shard_map/ppermute | solution.py:459
  19.9 45.4 %collective-permute-start = (bf16[272,384]{1,0:T(8,128)(2,1)}, bf16[272,384]{1,0:T(8,128)(2,1)}, u32[]{:S(2)}, u32[]{:S(2)}) collective-permute-start(bf16[272,384]{1,0:T(8,128)(2,1)} %get-tuple-element.28), channel_id=1, source_target_pairs={{0,1},{1,0},{2,3},{3,2},{4,5},{5,4},{6,7},{7,6},{8,9},{9,8},{10,11... | collective-permute-start | bytes 626696 | tf_op jit(solution)/shard_map/ppermute | solution.py:459
  57.2 0.9 copy-start
  58.2 17.4 %all-to-all-start.2 = ((bf16[4,4,64,384]{3,2,1,0:T(8,128)(2,1)}), bf16[4,4,64,384]{3,2,1,0:T(8,128)(2,1)}, u32[]{:S(2)}, u32[]{:S(2)}) async-start(bf16[4,4,64,384]{3,2,1,0:T(8,128)(2,1)} %copy-done), calls=%async_computation.2 | async-start | bytes 1572864 | tf_op jit(solution)/shard_map/all_to_all | solution.py:477
  68.8 0.9 copy-start.1
  72.2 1.1 copy-start.2
  75.5 43.1 %all-to-all-start.1 = ((bf16[4,4,64,384]{3,2,1,0:T(8,128)(2,1)}), bf16[4,4,64,384]{3,2,1,0:T(8,128)(2,1)}, u32[]{:S(2)}, u32[]{:S(2)}) async-start(bf16[4,4,64,384]{3,2,1,0:T(8,128)(2,1)} %copy-done.1), calls=%async_computation.1 | async-start | bytes 1572864 | tf_op jit(solution)/shard_map/all_to_all | solution.py:477
  82.8 1.3 copy-start.3
  118.6 1.3 copy-start.4
